TPU v7x, 256 devices: a whole 4x4x8 slice. The times are simulated.
256 devices in a mesh: tensor: 4 (over x), shard: 64 (over z, y, core).
Axes of the slice: x: 4, y: 4, z: 8, core: 2. Of those that a mesh axis runs over, the one named last changes fastest.
Arguments:
- proj_grads: bfloat16 [128, 2, 1152, 1024], P('shard', None, None, 'tensor'), may hold values from -60 to 60
- kv_grads: bfloat16 [512, 1152, 512], P(('tensor', 'shard')), may hold values from -60 to 60
- gain_grads: bfloat16 [512, 2, 256], P(('tensor', 'shard')), may hold values from -60 to 60
- proj_master: float32 [2, 1152, 1024], P(None, 'shard', 'tensor'), may hold values from -0.3125 to 0.3125
- proj_m: float32 [2, 1152, 1024], P(None, 'shard', 'tensor'), may hold values from -1.5 to 1.5
- proj_v: float32 [2, 1152, 1024], P(None, 'shard', 'tensor'), may hold values from 0.02 to 0.5
- kv_master: float32 [1152, 512], P('shard', 'tensor'), may hold values from -0.3125 to 0.3125
- kv_m: float32 [1152, 512], P('shard', 'tensor'), may hold values from -1.5 to 1.5
- kv_v: float32 [1152, 512], P('shard', 'tensor'), may hold values from 0.02 to 0.5
- gains: float32 [2, 256], replicated, may hold values from 0.1 to 1.9
- gains_m: float32 [2, 256], replicated, may hold values from -6 to 6
- gains_v: float32 [2, 256], replicated, may hold values from 0.25 to 4
Outputs:
- proj_master_new: float32 [2, 1152, 1024], P(None, 'shard', 'tensor')
- proj_m_new: float32 [2, 1152, 1024], P(None, 'shard', 'tensor')
- proj_v_new: float32 [2, 1152, 1024], P(None, 'shard', 'tensor')
- proj_weights: bfloat16 [2, 1152, 1024], P(None, None, 'tensor')
- kv_master_new: float32 [1152, 512], P('shard', 'tensor')
- kv_m_new: float32 [1152, 512], P('shard', 'tensor')
- kv_v_new: float32 [1152, 512], P('shard', 'tensor')
- kv_weights: bfloat16 [1152, 512], replicated
- gains_new: float32 [2, 256], replicated
- gains_m_new: float32 [2, 256], replicated
- gains_v_new: float32 [2, 256], replicated
All inputs are finite; a program needn't handle non-finite values.
Results may differ from a plain program's by a relative error of at most 0.0004.
Values may be sent and summed in bfloat16 or wider, within the bound.
A program may use at most 64 MiB of HBM per device.

v0:
```python
import math
import jax
import jax.numpy as jnp
from jax import lax
from jax.sharding import PartitionSpec as P

PARAMS = 2949632
beta_one = 0.9
beta_two = 0.95
learn_rate = 0.01
decay_rate = 0.1
epsilon = 1e-08
step_count = 10


def adamw_step(master, moment, second, update_grad, decay):
    moment_new = beta_one * moment + (1.0 - beta_one) * update_grad
    second_new = beta_two * second + (1.0 - beta_two) * update_grad * update_grad
    first_hat = moment_new / (1.0 - beta_one**step_count)
    second_hat = second_new / (1.0 - beta_two**step_count)
    master_new = master - learn_rate * (
        first_hat / (jnp.sqrt(second_hat) + epsilon) + decay * master
    )
    return (master_new, moment_new, second_new)


def shards(
    proj_grads,
    kv_grads,
    gain_grads,
    proj_master,
    proj_m,
    proj_v,
    kv_master,
    kv_m,
    kv_v,
    gains,
    gains_m,
    gains_v,
):
    proj_local = jnp.sum(proj_grads, axis=0, dtype=jnp.float32)
    kv_local = jnp.sum(kv_grads, axis=0, dtype=jnp.float32)
    gain_local = jnp.sum(gain_grads, axis=0, dtype=jnp.float32)
    gain_sum = lax.psum(gain_local, ("tensor", "shard"))
    proj_owned, kv_row_part = (
        lax.psum_scatter(proj_local, "shard", scatter_dimension=1, tiled=True),
        lax.psum_scatter(kv_local, "shard", scatter_dimension=0, tiled=True),
    )
    kv_owned = lax.psum_scatter(kv_row_part, "tensor", scatter_dimension=1, tiled=True)
    owned_square = jnp.sum(proj_owned * proj_owned) + jnp.sum(kv_owned * kv_owned)
    norm_square = lax.psum(owned_square, ("tensor", "shard")) + jnp.sum(gain_sum * gain_sum)
    clip_factor = jnp.minimum(1.0, math.sqrt(PARAMS) / jnp.sqrt(norm_square))
    proj_new, proj_m_new, proj_v_new = adamw_step(
        proj_master, proj_m, proj_v, clip_factor * proj_owned, decay_rate
    )
    kv_new, kv_m_new, kv_v_new = adamw_step(
        kv_master, kv_m, kv_v, clip_factor * kv_owned, decay_rate
    )
    gains_new, gains_m_new, gains_v_new = adamw_step(
        gains, gains_m, gains_v, clip_factor * gain_sum, 0.0
    )
    proj_half = proj_new.astype(jnp.bfloat16)
    kv_half = kv_new.astype(jnp.bfloat16)
    kv_wide = lax.all_gather(kv_half, "tensor", axis=1, tiled=True)
    proj_weights, kv_weights = (
        lax.all_gather(proj_half, "shard", axis=1, tiled=True),
        lax.all_gather(kv_wide, "shard", axis=0, tiled=True),
    )
    return (
        proj_new,
        proj_m_new,
        proj_v_new,
        proj_weights,
        kv_new,
        kv_m_new,
        kv_v_new,
        kv_weights,
        gains_new,
        gains_m_new,
        gains_v_new,
    )


def solution(mesh):
    placed = (
        P("shard", None, None, "tensor"),
        P(("tensor", "shard"), None, None),
        P(("tensor", "shard"), None, None),
        P(None, "shard", "tensor"),
        P(None, "shard", "tensor"),
        P(None, "shard", "tensor"),
        P("shard", "tensor"),
        P("shard", "tensor"),
        P("shard", "tensor"),
        P(),
        P(),
        P(),
    )
    return jax.shard_map(
        shards,
        mesh=mesh,
        in_specs=placed,
        out_specs=(
            P(None, "shard", "tensor"),
            P(None, "shard", "tensor"),
            P(None, "shard", "tensor"),
            P(None, None, "tensor"),
            P("shard", "tensor"),
            P("shard", "tensor"),
            P("shard", "tensor"),
            P(),
            P(),
            P(),
            P(),
        ),
        check_vma=False,
    )
```

profile of v0, /device:TPU:1, one launch (start us, length us, event | category | flops | bytes accessed | tf_op | source)
XLA Modules:
  0.0 487.7 jit_solution(7765557723649341525)
XLA Ops:
  7.2 0.0 all-reduce.6.cloned.1.call-start
  7.2 2.3 convert_reduce_fusion.1
  9.5 0.0 copy-start
  9.5 7.6 %copy.25 = f32[2,1152,256]{2,0,1:T(2,128)} copy(f32[2,1152,256]{2,1,0:T(8,128)S(1)} %convert_reduce_fusion.1) | data formatting | bytes 4718592 | tf_op jit(solution)/shard_map/reduce_sum | solution.py:41
  17.2 2.0 convert_reduce_fusion
  19.2 0.0 copy-start.4
  19.2 0.0 copy-start.6
  19.2 0.0 copy-start.8
  19.3 0.0 all-reduce.6.cloned.1.call-update
  19.3 0.0 reduce-scatter.2.cloned.1.call-start
  19.3 0.5 copy-done.11
  19.9 0.6 dynamic-slice
  21.1 197.5 %all-reduce.6.cloned.1.call-done = (f32[2,1152,256]{2,0,1:T(2,128)}, f32[1152,512]{1,0:T(8,128)}) async-done(((f32[2,1152,256]{2,0,1:T(2,128)}, f32[1152,512]{1,0:T(8,128)}), (f32[2,1152,256]{2,0,1:T(2,128)}, f32[1152,512]{1,0:T(8,128)})) %all-reduce.6.cloned.1.call-update) | async-done | bytes 4718608
  218.6 1.5 constant_dynamic-slice_fusion
  220.1 0.0 reduce-scatter.2.cloned.1.call-update
  220.1 0.0 all-gather.4.cloned.1.call-start
  220.2 1.4 multiply_reduce_fusion
  221.6 21.1 %reduce-scatter.2.cloned.1.call-done = f32[18,128]{1,0:T(8,128)} async-done(((f32[18,512]{1,0:T(8,128)}), f32[18,128]{1,0:T(8,128)}) %reduce-scatter.2.cloned.1.call-update) | async-done | bytes 9232 | tf_op jit(solution)/shard_map/reduce_scatter | solution.py:49
  242.7 1.3 multiply_reduce_fusion.1
  245.3 78.1 %all-reduce.2 = (f32[]{:T(128)}, f32[2,256]{1,0:T(2,128)S(1)}) all-reduce(f32[]{:T(128)S(6)} %add.61, f32[2,256]{1,0:T(2,128)S(1)} %convert_reduce_fusion.2), channel_id=1, replica_groups=mesh['tensor'=4,'shard'=64] {'tensor','shard'}, use_global_device_ids=true, to_apply=%region_7.0 | all-reduce | flops 513 | bytes 4104 | tf_op jit(solution)/shard_map/psum | solution.py:51
  323.5 0.6 multiply_reduce_fusion.2
  325.4 1.5 fusion.6
  327.0 0.0 all-gather.4.cloned.1.call-update
  327.0 0.0 all-gather.6.cloned.1.call-start
  327.1 1.3 fusion.4
  328.4 8.5 %all_gather.10 = bf16[18,512]{1,0:T(8,128)(2,1)} all-gather(bf16[18,128]{1,0:T(8,128)(2,1)S(1)} %get-tuple-element.29), channel_id=1, replica_groups=mesh['tensor'=4,'shard'=64] {'tensor'}, dimensions={1}, use_global_device_ids=true | all-gather | bytes 23040 | tf_op jit(solution)/shard_map/all_gather | solution.py:64
  336.9 0.0 all-gather.6.cloned.1.call-update
  336.9 0.6 multiply_subtract_fusion.2
  337.5 63.2 %all-gather.4.cloned.1.call-done = bf16[2,1152,256]{2,0,1:T(2,128)(2,1)} async-done(((bf16[2,18,256]{2,0,1:T(2,128)(2,1)}), bf16[2,1152,256]{2,0,1:T(2,128)(2,1)}) %all-gather.4.cloned.1.call-update) | async-done | bytes 1179664 | tf_op jit(solution)/shard_map/all_gather | solution.py:66
  400.7 2.4 copy.26
  403.2 74.9 %all-gather.6.cloned.1.call-done = bf16[64,18,512]{2,1,0:T(8,128)(2,1)} async-done(((bf16[1,18,512]{2,1,0:T(8,128)(2,1)}), bf16[64,18,512]{2,1,0:T(8,128)(2,1)}) %all-gather.6.cloned.1.call-update) | async-done | bytes 1179664 | tf_op jit(solution)/shard_map/all_gather | solution.py:67
  478.1 3.1 reshape.23
  (20 shorter events, 0.1 us)
Async XLA Ops:
  7.2 211.4 %all-reduce.6.cloned.1.call-start = ((), (), s32[]{:S(2)}) async-start(), calls=%async_computation.4 | async-start | bytes 9437184
  9.5 7.7 %copy-start = (bf16[2,1152,512]{2,1,0:T(8,128)(2,1)S(1)}, bf16[2,1152,512]{2,1,0:T(8,128)(2,1)}, u32[]{:S(2)}) copy-start(bf16[2,1152,512]{2,1,0:T(8,128)(2,1)} %param.13) | copy-start | bytes 7077892
  19.2 0.7 copy-start.11
  19.2 201.0 %copy-start.7 = (bf16[2,2,256]{2,1,0:T(2,128)(2,1)S(1)}, bf16[2,2,256]{2,1,0:T(2,128)(2,1)}, u32[]{:S(2)}) copy-start(bf16[2,2,256]{2,1,0:T(2,128)(2,1)} %param.14) | copy-start | bytes 6148
  19.2 306.2 %copy-start.1 = (f32[2,18,256]{2,0,1:T(2,128)S(1)}, f32[2,18,256]{2,0,1:T(2,128)}, u32[]{:S(2)}) copy-start(f32[2,18,256]{2,0,1:T(2,128)} %param.15) | copy-start | bytes 110596
  19.2 306.2 %copy-start.2 = (f32[2,18,256]{2,0,1:T(2,128)S(1)}, f32[2,18,256]{2,0,1:T(2,128)}, u32[]{:S(2)}) copy-start(f32[2,18,256]{2,0,1:T(2,128)} %param.16) | copy-start | bytes 110596
  19.2 306.2 %copy-start.3 = (f32[2,18,256]{2,0,1:T(2,128)S(1)}, f32[2,18,256]{2,0,1:T(2,128)}, u32[]{:S(2)}) copy-start(f32[2,18,256]{2,0,1:T(2,128)} %param.17) | copy-start | bytes 110596
  19.2 307.9 %copy-start.4 = (f32[18,128]{1,0:T(8,128)S(1)}, f32[18,128]{1,0:T(8,128)}, u32[]{:S(2)}) copy-start(f32[18,128]{1,0:T(8,128)} %param.18) | copy-start | bytes 27652
  19.2 307.9 %copy-start.5 = (f32[18,128]{1,0:T(8,128)S(1)}, f32[18,128]{1,0:T(8,128)}, u32[]{:S(2)}) copy-start(f32[18,128]{1,0:T(8,128)} %param.19) | copy-start | bytes 27652
  19.2 307.9 %copy-start.6 = (f32[18,128]{1,0:T(8,128)S(1)}, f32[18,128]{1,0:T(8,128)}, u32[]{:S(2)}) copy-start(f32[18,128]{1,0:T(8,128)} %param.20) | copy-start | bytes 27652
  19.2 317.7 %copy-start.8 = (f32[2,256]{1,0:T(2,128)S(1)}, f32[2,256]{1,0:T(2,128)}, u32[]{:S(2)}) copy-start(f32[2,256]{1,0:T(2,128)} %param.21) | copy-start | bytes 6148
  19.2 317.7 %copy-start.9 = (f32[2,256]{1,0:T(2,128)S(1)}, f32[2,256]{1,0:T(2,128)}, u32[]{:S(2)}) copy-start(f32[2,256]{1,0:T(2,128)} %param.22) | copy-start | bytes 6148
  19.3 317.7 %copy-start.10 = (f32[2,256]{1,0:T(2,128)S(1)}, f32[2,256]{1,0:T(2,128)}, u32[]{:S(2)}) copy-start(f32[2,256]{1,0:T(2,128)} %param.23) | copy-start | bytes 6148
  19.3 223.4 %reduce-scatter.2.cloned.1.call-start = ((), (), s32[]{:S(2)}) async-start(), calls=%async_computation.1 | async-start | bytes 61440 | tf_op jit(solution)/shard_map/reduce_scatter | solution.py:49
  220.1 180.6 %all-gather.4.cloned.1.call-start = ((), (), s32[]{:S(2)}) async-start(), calls=%async_computation.2 | async-start | bytes 1198080 | tf_op jit(solution)/shard_map/all_gather | solution.py:66
  327.0 151.1 %all-gather.6.cloned.1.call-start = ((), (), s32[]{:S(2)}) async-start(), calls=%async_computation.3 | async-start | bytes 1597440 | tf_op jit(solution)/shard_map/all_gather | solution.py:67
Sparse Core Ops, SparseCore 0:
  19.4 199.1 all-reduce.5
  221.8 20.8 reduce-scatter.1
  327.1 73.5 all-gather.3
  403.4 74.6 all-gather.5
where the time goes:
time: 488 us
  waiting for transfers between devices  357 us (73%)
  blocking collectives  86.6 us (18%)
  between operations  17.2 us (4%)
  local copies, waits for them, and re-layouts  15.8 us (3%)
  other arithmetic  11.1 us (2%)
    unnamed x5, waiting for transfers between devices  198 us
    psum x1, blocking collectives, shards(): lax.psum(owned_square, ('tensor', 'shard')) + jnp.sum(gain_sum * gain_sum)  78.1 us
    all_gather x1, waiting for transfers between devices, shards(): lax.all_gather(kv_wide, 'shard', axis=0, tiled=True)  74.9 us
    all_gather x1, waiting for transfers between devices, shards(): lax.all_gather(proj_half, 'shard', axis=1, tiled=True)  63.2 us
    reduce_scatter x1, waiting for transfers between devices, shards(): lax.psum_scatter(kv_row_part, 'tensor', scatter_dimension=1, tiled=True)  21.1 us
  transfers between devices with their start and end apart: 4, of which 4 were waited for; matrix products, arithmetic and copies ran while one was open for 1% of the time, Pallas kernels for 0%

commit v1 on v0

--- a/solution.py
+++ b/solution.py
@@ -63,7 +63,9 @@
     kv_half = kv_new.astype(jnp.bfloat16)
     kv_wide = lax.all_gather(kv_half, "tensor", axis=1, tiled=True)
     proj_weights, kv_weights = (
-        lax.all_gather(proj_half, "shard", axis=1, tiled=True),
+        jnp.concatenate(
+            lax.all_to_all(jnp.stack([proj_half] * lax.axis_size("shard")), "shard", 0, 0), axis=1
+        ),
         lax.all_gather(kv_wide, "shard", axis=0, tiled=True),
     )
     return (

time: 488 us -> 436 us (0.89)
  waiting for transfers between devices: 357 us -> 297 us
  starting transfers between devices: 0.16 us -> 7.72 us
    all_gather x1 -> x0, waiting for transfers between devices: 63.2 us -> none  [shards(): lax.all_gather(proj_half, 'shard', axis=1, tiled=True)]
    all_to_all x0 -> x1, waiting for transfers between devices: none -> 20.2 us  [shards(): lax.all_to_all(jnp.stack([proj_half] * lax.axis_size('shard')), 'shard',...]
    all_gather x1, waiting for transfers between devices: 74.9 us -> 57.9 us  [shards(): lax.all_gather(kv_wide, 'shard', axis=0, tiled=True)]
    all_to_all x0 -> x1, starting transfers between devices: none -> 7.6 us  [shards(): lax.all_to_all(jnp.stack([proj_half] * lax.axis_size('shard')), 'shard',...]
    unnamed x5 -> x4, waiting for transfers between devices: 198 us -> 197 us
where the time goes in v1:
time: 436 us
  waiting for transfers between devices  297 us (68%)
  blocking collectives  87.1 us (20%)
  between operations  17.2 us (4%)
  local copies, waits for them, and re-layouts  16.1 us (4%)
  other arithmetic  10.5 us (2%)
  starting transfers between devices  7.72 us (2%)
    unnamed x4, waiting for transfers between devices  197 us
    psum x1, blocking collectives, shards(): lax.psum(owned_square, ('tensor', 'shard')) + jnp.sum(gain_sum * gain_sum)  78.1 us
    all_gather x1, waiting for transfers between devices, shards(): lax.all_gather(kv_wide, 'shard', axis=0, tiled=True)  57.9 us
    reduce_scatter x1, waiting for transfers between devices, shards(): lax.psum_scatter(kv_row_part, 'tensor', scatter_dimension=1, tiled=True)  21.2 us
    all_to_all x1, waiting for transfers between devices, shards(): lax.all_to_all(jnp.stack([proj_half] * lax.axis_size('shard')), 'shard',...  20.2 us
    all_gather x1, blocking collectives, shards(): kv_wide = lax.all_gather(kv_half, 'tensor', axis=1, tiled=True)  9.01 us
  transfers between devices with their start and end apart: 4, of which 4 were waited for; matrix products, arithmetic and copies ran while one was open for 1% of the time, Pallas kernels for 0%

profile of v1, /device:TPU:1, one launch (start us, length us, event | category | flops | bytes accessed | tf_op | source)
XLA Modules:
  0.0 435.5 jit_solution(13094088748155352786)
XLA Ops:
  7.2 0.0 all-reduce.6.cloned.1.call-start
  7.2 2.3 convert_reduce_fusion.1
  9.6 0.0 copy-start
  9.6 7.6 %copy.25 = f32[2,1152,256]{2,0,1:T(2,128)} copy(f32[2,1152,256]{2,1,0:T(8,128)S(1)} %convert_reduce_fusion.1) | data formatting | bytes 4718592 | tf_op jit(solution)/shard_map/reduce_sum | solution.py:41
  17.2 2.0 convert_reduce_fusion
  19.2 0.0 all-reduce.6.cloned.1.call-update
  19.3 0.0 copy-start.6
  19.3 0.0 copy-start.7
  19.3 0.0 copy-start.11
  19.3 0.0 reduce-scatter.2.cloned.1.call-start
  19.4 0.5 copy-done.12
  19.9 0.6 dynamic-slice
  21.1 197.4 %all-reduce.6.cloned.1.call-done = (f32[2,1152,256]{2,0,1:T(2,128)}, f32[1152,512]{1,0:T(8,128)}) async-done(((f32[2,1152,256]{2,0,1:T(2,128)}, f32[1152,512]{1,0:T(8,128)}), (f32[2,1152,256]{2,0,1:T(2,128)}, f32[1152,512]{1,0:T(8,128)})) %all-reduce.6.cloned.1.call-update) | async-done | bytes 4718608
  218.6 1.5 constant_dynamic-slice_fusion
  220.0 0.0 reduce-scatter.2.cloned.1.call-update
  220.1 1.4 multiply_reduce_fusion
  221.5 21.2 %reduce-scatter.2.cloned.1.call-done = f32[18,128]{1,0:T(8,128)} async-done(((f32[18,512]{1,0:T(8,128)}), f32[18,128]{1,0:T(8,128)}) %reduce-scatter.2.cloned.1.call-update) | async-done | bytes 9232 | tf_op jit(solution)/shard_map/reduce_scatter | solution.py:49
  242.7 1.4 multiply_reduce_fusion.1
  245.4 78.1 %all-reduce.2 = (f32[]{:T(128)}, f32[2,256]{1,0:T(2,128)S(1)}) all-reduce(f32[]{:T(128)S(6)} %add.61, f32[2,256]{1,0:T(2,128)S(1)} %convert_reduce_fusion.2), channel_id=1, replica_groups=mesh['tensor'=4,'shard'=64] {'tensor','shard'}, use_global_device_ids=true, to_apply=%region_7.0 | all-reduce | flops 513 | bytes 4104 | tf_op jit(solution)/shard_map/psum | solution.py:51
  323.5 0.6 multiply_reduce_fusion.2
  325.5 1.5 fusion.6
  327.0 1.6 stack.2
  328.6 7.6 %all-to-all-start = ((bf16[64,2,18,256]{3,1,2,0:T(2,128)(2,1)}), bf16[64,2,18,256]{3,1,2,0:T(2,128)(2,1)S(1)}, u32[]{:S(2)}, u32[]{:S(2)}) async-start(bf16[64,2,18,256]{3,1,2,0:T(2,128)(2,1)} %stack.2), calls=%async_computation.1 | async-start | bytes 2359296 | tf_op jit(solution)/shard_map/all_to_all | solution.py:67
  336.2 0.0 all-gather.3.cloned.1.call-start
  336.3 0.6 fusion.4
  337.0 9.0 %all_gather.6 = bf16[18,512]{1,0:T(8,128)(2,1)} all-gather(bf16[18,128]{1,0:T(8,128)(2,1)S(1)} %get-tuple-element.40), channel_id=1, replica_groups=mesh['tensor'=4,'shard'=64] {'tensor'}, dimensions={1}, use_global_device_ids=true | all-gather | bytes 23040 | tf_op jit(solution)/shard_map/all_gather | solution.py:64
  346.0 0.0 all-gather.3.cloned.1.call-update
  346.0 0.6 multiply_subtract_fusion.2
  346.6 20.2 %all-to-all-done = bf16[64,2,18,256]{3,1,2,0:T(2,128)(2,1)S(1)} async-done(((bf16[64,2,18,256]{3,1,2,0:T(2,128)(2,1)}), bf16[64,2,18,256]{3,1,2,0:T(2,128)(2,1)S(1)}, u32[]{:S(2)}, u32[]{:S(2)}) %all-to-all-start) | async-done | bytes 1179680 | tf_op jit(solution)/shard_map/all_to_all | solution.py:67
  366.8 1.2 copy.26
  368.0 57.9 %all-gather.3.cloned.1.call-done = bf16[64,18,512]{2,1,0:T(8,128)(2,1)} async-done(((bf16[1,18,512]{2,1,0:T(8,128)(2,1)}), bf16[64,18,512]{2,1,0:T(8,128)(2,1)}) %all-gather.3.cloned.1.call-update) | async-done | bytes 1179664 | tf_op jit(solution)/shard_map/all_gather | solution.py:69
  425.9 3.1 reshape.33
  (22 shorter events, 0.1 us)
Async XLA Ops:
  7.2 211.4 %all-reduce.6.cloned.1.call-start = ((), (), s32[]{:S(2)}) async-start(), calls=%async_computation.4 | async-start | bytes 9437184
  9.6 7.7 %copy-start = (bf16[2,1152,512]{2,1,0:T(8,128)(2,1)S(1)}, bf16[2,1152,512]{2,1,0:T(8,128)(2,1)}, u32[]{:S(2)}) copy-start(bf16[2,1152,512]{2,1,0:T(8,128)(2,1)} %param.13) | copy-start | bytes 7077892
  19.2 0.7 copy-start.12
  19.2 200.8 %copy-start.8 = (bf16[2,2,256]{2,1,0:T(2,128)(2,1)S(1)}, bf16[2,2,256]{2,1,0:T(2,128)(2,1)}, u32[]{:S(2)}) copy-start(bf16[2,2,256]{2,1,0:T(2,128)(2,1)} %param.14) | copy-start | bytes 6148
  19.2 306.2 %copy-start.2 = (f32[2,18,256]{2,0,1:T(2,128)S(1)}, f32[2,18,256]{2,0,1:T(2,128)}, u32[]{:S(2)}) copy-start(f32[2,18,256]{2,0,1:T(2,128)} %param.15) | copy-start | bytes 110596
  19.2 306.2 %copy-start.3 = (f32[2,18,256]{2,0,1:T(2,128)S(1)}, f32[2,18,256]{2,0,1:T(2,128)}, u32[]{:S(2)}) copy-start(f32[2,18,256]{2,0,1:T(2,128)} %param.16) | copy-start | bytes 110596
  19.2 306.2 %copy-start.4 = (f32[2,18,256]{2,0,1:T(2,128)S(1)}, f32[2,18,256]{2,0,1:T(2,128)}, u32[]{:S(2)}) copy-start(f32[2,18,256]{2,0,1:T(2,128)} %param.17) | copy-start | bytes 110596
  19.3 317.0 %copy-start.5 = (f32[18,128]{1,0:T(8,128)S(1)}, f32[18,128]{1,0:T(8,128)}, u32[]{:S(2)}) copy-start(f32[18,128]{1,0:T(8,128)} %param.18) | copy-start | bytes 27652
  19.3 317.0 %copy-start.6 = (f32[18,128]{1,0:T(8,128)S(1)}, f32[18,128]{1,0:T(8,128)}, u32[]{:S(2)}) copy-start(f32[18,128]{1,0:T(8,128)} %param.19) | copy-start | bytes 27652
  19.3 317.0 %copy-start.7 = (f32[18,128]{1,0:T(8,128)S(1)}, f32[18,128]{1,0:T(8,128)}, u32[]{:S(2)}) copy-start(f32[18,128]{1,0:T(8,128)} %param.20) | copy-start | bytes 27652
  19.3 326.7 %copy-start.9 = (f32[2,256]{1,0:T(2,128)S(1)}, f32[2,256]{1,0:T(2,128)}, u32[]{:S(2)}) copy-start(f32[2,256]{1,0:T(2,128)} %param.21) | copy-start | bytes 6148
  19.3 326.7 %copy-start.10 = (f32[2,256]{1,0:T(2,128)S(1)}, f32[2,256]{1,0:T(2,128)}, u32[]{:S(2)}) copy-start(f32[2,256]{1,0:T(2,128)} %param.22) | copy-start | bytes 6148
  19.3 326.7 %copy-start.11 = (f32[2,256]{1,0:T(2,128)S(1)}, f32[2,256]{1,0:T(2,128)}, u32[]{:S(2)}) copy-start(f32[2,256]{1,0:T(2,128)} %param.23) | copy-start | bytes 6148
  19.3 223.4 %reduce-scatter.2.cloned.1.call-start = ((), (), s32[]{:S(2)}) async-start(), calls=%async_computation.2 | async-start | bytes 61440 | tf_op jit(solution)/shard_map/reduce_scatter | solution.py:49
  242.7 93.6 %copy-start.1 = (f32[18,128]{1,0:T(8,128)S(1)}, f32[18,128]{1,0:T(8,128)}, u32[]{:S(2)}) copy-start(f32[18,128]{1,0:T(8,128)} %reduce-scatter.2.cloned.1.call-done) | copy-start | bytes 27652
  328.6 38.2 %all-to-all-start = ((bf16[64,2,18,256]{3,1,2,0:T(2,128)(2,1)}), bf16[64,2,18,256]{3,1,2,0:T(2,128)(2,1)S(1)}, u32[]{:S(2)}, u32[]{:S(2)}) async-start(bf16[64,2,18,256]{3,1,2,0:T(2,128)(2,1)} %stack.2), calls=%async_computation.1 | async-start | bytes 2359296 | tf_op jit(solution)/shard_map/all_to_all | solution.py:67
  336.2 89.7 %all-gather.3.cloned.1.call-start = ((), (), s32[]{:S(2)}) async-start(), calls=%async_computation.3 | async-start | bytes 1597440 | tf_op jit(solution)/shard_map/all_gather | solution.py:69
Sparse Core Ops, SparseCore 0:
  19.4 199.1 all-reduce.5
  221.8 20.8 reduce-scatter.1
  346.1 79.7 all-gather.2
